TPU v7x, 512 devices: a whole 4x8x8 slice. The times are simulated.
512 devices in a mesh: plane: 32 (over x, z), tile: 16 (over y, core).
Axes of the slice: x: 4, y: 8, z: 8, core: 2. Of those that a mesh axis runs over, the one named last changes fastest.
Arguments:
- raw_planes: bfloat16 [3072, 512, 512], P('plane', 'tile'), may hold values from -6 to 6
- pair_sections: int32 [2048, 2], P('plane'), may hold values from 0 to 47
- pair_rows: int32 [2048, 2], P('plane'), may hold values from 0 to 128
- pair_extent: int32 [2048], P('plane'), may hold values from 64 to 128
- pair_owner: int32 [2048, 1], P('plane'), may hold values from 0 to 15; in each aligned block of 64 rows (0 to 63, 64 to 127, ...) at most 12 rows name the same one
Outputs:
- surface_out: bfloat16 [6144, 128, 256], P(('plane', 'tile'))
Inputs may be any that keep to these rules, and one draw needn't show every extreme that they name: `pair_owner`: among the 64 pairs of one slab no owner takes more than 12 pairs.
All inputs are finite; a program needn't handle non-finite values.
Results may differ from a plain program's by a relative error of at most 0.012.
The roundings to bfloat16 on the way count: a program that leaves them out, or rounds other values in their place, can miss the bound.
Values may be sent and summed in bfloat16 or wider, within the bound.
No kernel may reach another device: no remote copies, remote signals or barrier semaphores. Data moves between devices by JAX's collectives and lax.ppermute only.
A program may use at most 64 MiB of HBM per device.

v0:
```python
import math
import jax
import jax.numpy as jnp
from jax import lax
from jax.sharding import PartitionSpec as P

BAND = 128
OWN_CAP = 12


def from_behind(value, axis, steps):
    count = lax.axis_size(axis)
    initial, last = (max(0, -steps), min(count, count - steps))
    return lax.ppermute(value, axis, [(source, source + steps) for source in range(initial, last)])


def blur_matrix(face_cells, half_cells):
    source = jnp.arange(face_cells, dtype=jnp.int32)[:, None]
    target = jnp.arange(half_cells, dtype=jnp.int32)[None, :]
    offset = jnp.abs(source - 2 * target)
    weights = jnp.where(
        offset == 0, 6.0, jnp.where(offset == 1, 4.0, jnp.where(offset == 2, 1.0, 0.0))
    )
    return (weights * 0.0625).astype(jnp.bfloat16)


def dft_tables(length):
    indices = jnp.arange(length, dtype=jnp.int32)
    phases = indices[:, None] * indices[None, :] % length
    angles = phases.astype(jnp.float32) * (2.0 * math.pi / length)
    factor = 1.0 / math.sqrt(length)
    return (
        (jnp.cos(angles) * factor).astype(jnp.bfloat16),
        (jnp.sin(angles) * factor).astype(jnp.bfloat16),
    )


def correlate(first_bands, second_bands):
    pair_count = first_bands.shape[0]
    band_rows = first_bands.shape[1]
    columns = first_bands.shape[2]
    cos_half, sin_half = dft_tables(columns)
    cos_band, sin_band = dft_tables(band_rows)
    stacked = jnp.concatenate([first_bands, second_bands], axis=0).reshape(
        2 * pair_count * band_rows, columns
    )
    forward_table = jnp.concatenate([cos_half, -sin_half], axis=1)
    rowwise = jnp.dot(stacked, forward_table, preferred_element_type=jnp.float32).astype(
        jnp.bfloat16
    )
    rowwise = rowwise.reshape(2 * pair_count, band_rows, 2 * columns)
    row_real = rowwise[:, :, :columns]
    row_imag = rowwise[:, :, columns:]
    spec_real = jnp.einsum(
        "uv,kvj->kuj", cos_band, row_real, preferred_element_type=jnp.float32
    ) + jnp.einsum("uv,kvj->kuj", sin_band, row_imag, preferred_element_type=jnp.float32)
    spec_imag = jnp.einsum(
        "uv,kvj->kuj", cos_band, row_imag, preferred_element_type=jnp.float32
    ) - jnp.einsum("uv,kvj->kuj", sin_band, row_real, preferred_element_type=jnp.float32)
    first_real = spec_real[:pair_count]
    first_imag = spec_imag[:pair_count]
    second_real = spec_real[pair_count:]
    second_imag = spec_imag[pair_count:]
    cross_real = first_real * second_real + first_imag * second_imag
    cross_imag = first_imag * second_real - first_real * second_imag
    magnitude = jnp.sqrt(cross_real * cross_real + cross_imag * cross_imag)
    mean_level = jnp.mean(magnitude, axis=(1, 2), keepdims=True) + 1e-06
    divisor = magnitude + mean_level
    norm_real = (cross_real / divisor).astype(jnp.bfloat16)
    norm_imag = (cross_imag / divisor).astype(jnp.bfloat16)
    col_real = (
        jnp.einsum("uv,kvj->kuj", cos_band, norm_real, preferred_element_type=jnp.float32)
        - jnp.einsum("uv,kvj->kuj", sin_band, norm_imag, preferred_element_type=jnp.float32)
    ).astype(jnp.bfloat16)
    col_imag = (
        jnp.einsum("uv,kvj->kuj", cos_band, norm_imag, preferred_element_type=jnp.float32)
        + jnp.einsum("uv,kvj->kuj", sin_band, norm_real, preferred_element_type=jnp.float32)
    ).astype(jnp.bfloat16)
    joined = jnp.concatenate([col_real, col_imag], axis=2).reshape(
        pair_count * band_rows, 2 * columns
    )
    inverse_table = jnp.concatenate([cos_half, -sin_half], axis=0)
    surface = jnp.dot(joined, inverse_table, preferred_element_type=jnp.float32)
    return surface.reshape(pair_count, band_rows, columns).astype(jnp.bfloat16)


def fetch_bands(sections, section_ids, first_rows, extents):
    wanted = section_ids.shape[0]
    columns = sections.shape[2]
    zero_index = jnp.zeros((), jnp.int32)
    blank_bands = jnp.zeros((wanted, BAND, columns), sections.dtype)
    band_index = jnp.arange(BAND, dtype=jnp.int32)
    shards = lax.all_gather(sections, "tile", axis=0, tiled=True)
    held = shards.shape[0]
    inside = (section_ids >= 0) & (section_ids < held)
    clipped = jnp.clip(section_ids, 0, held - 1)

    def slice_band(which, row_start):
        return lax.dynamic_slice(shards, (which, row_start, zero_index), (1, BAND, columns))[0]

    cutout = jax.vmap(slice_band)(clipped, first_rows)
    bands = jnp.where(inside[:, None, None], cutout, blank_bands)
    live_rows = band_index[None, :, None] < extents[:, None, None]
    return jnp.where(live_rows, bands, jnp.zeros_like(bands))


def pair_bands(sections, pair_sections, pair_rows, pair_extent, chosen):
    picked_ids = jnp.take(pair_sections, chosen, axis=0)
    picked_rows = jnp.take(pair_rows, chosen, axis=0)
    picked_extent = jnp.take(pair_extent, chosen, axis=0)
    section_ids = jnp.concatenate([picked_ids[:, 0], picked_ids[:, 1]], axis=0)
    first_rows = jnp.concatenate([picked_rows[:, 0], picked_rows[:, 1]], axis=0)
    extents = jnp.concatenate([picked_extent, picked_extent], axis=0)
    bands = fetch_bands(sections, section_ids, first_rows, extents)
    pair_count = chosen.shape[0]
    return (bands[:pair_count], bands[pair_count:])


def depth_blur(planar, carried):
    count = planar.shape[0]
    previous = jnp.concatenate([carried[None], planar[: count - 1]], axis=0)
    return (
        (
            previous[0::2].astype(jnp.float32)
            + 2.0 * planar[0::2].astype(jnp.float32)
            + planar[1::2].astype(jnp.float32)
        )
        * 0.25
    ).astype(jnp.bfloat16)


def per_device(raw_planes, pair_sections, pair_rows, pair_extent, pair_owner):
    tile_count = lax.axis_size("tile")
    face_cells = raw_planes.shape[2]
    half_cells = face_cells // 2
    slab_planes = raw_planes.shape[0]
    planes_dev = slab_planes // tile_count
    blur_table = blur_matrix(face_cells, half_cells)
    regrouped = lax.all_to_all(raw_planes, "tile", split_axis=0, concat_axis=1, tiled=True)
    across = jnp.dot(
        regrouped.reshape(planes_dev * face_cells, face_cells),
        blur_table,
        preferred_element_type=jnp.float32,
    )
    across = across.astype(jnp.bfloat16).reshape(planes_dev, face_cells, half_cells)
    planar = jnp.einsum(
        "ri,zrj->zij", blur_table, across, preferred_element_type=jnp.float32
    ).astype(jnp.bfloat16)
    carried = from_behind(planar[planes_dev - 1], ("plane", "tile"), 1)
    sections = depth_blur(planar, carried)
    my_tile = lax.axis_index("tile")
    owners = pair_owner[:, 0]
    listed = owners.shape[0]
    position = jnp.arange(listed, dtype=jnp.int32)
    earlier = (owners[:, None] == owners[None, :]) & (position[None, :] < position[:, None])
    slot_of = jnp.sum(earlier.astype(jnp.int32), axis=1)
    slot_ids = jnp.arange(OWN_CAP, dtype=jnp.int32)
    picked = (owners[None, :] == my_tile) & (slot_of[None, :] == slot_ids[:, None])
    chosen = jnp.sum(jnp.where(picked, position[None, :], 0), axis=1)
    filled = jnp.any(picked, axis=1)
    first_bands, second_bands = pair_bands(sections, pair_sections, pair_rows, pair_extent, chosen)
    surfaces = correlate(first_bands, second_bands)
    return jnp.where(filled[:, None, None], surfaces, jnp.zeros_like(surfaces))


def solution(mesh):
    return jax.shard_map(
        per_device,
        mesh=mesh,
        in_specs=(
            P("plane", "tile", None),
            P("plane", None),
            P("plane", None),
            P("plane"),
            P("plane", None),
        ),
        out_specs=P(("plane", "tile"), None, None),
        check_vma=False,
    )
```

profile of v0, /device:TPU:1, one launch (start us, length us, event | category | flops | bytes accessed | tf_op | source)
XLA Modules:
  0.0 185.8 jit_solution(15391342763990343113)
XLA Ops:
  6.5 0.0 copy-start
  6.5 10.5 %all-to-all-start = ((bf16[96,32,512]{2,1,0:T(8,128)(2,1)}), bf16[96,32,512]{2,1,0:T(8,128)(2,1)S(1)}, u32[]{:S(2)}, u32[]{:S(2)}) async-start(bf16[96,32,512]{2,1,0:T(8,128)(2,1)} %param.7), calls=%async_computation | async-start | bytes 6291456 | tf_op jit(solution)/shard_map/all_to_all | solution.py:139
  17.0 0.0 all-gather.2.cloned.1.call-start
  17.1 70.9 %all-to-all-done = bf16[96,32,512]{2,1,0:T(8,128)(2,1)S(1)} async-done(((bf16[96,32,512]{2,1,0:T(8,128)(2,1)}), bf16[96,32,512]{2,1,0:T(8,128)(2,1)S(1)}, u32[]{:S(2)}, u32[]{:S(2)}) %all-to-all-start) | async-done | bytes 3145760 | tf_op jit(solution)/shard_map/all_to_all | solution.py:139
  88.0 0.2 copy.46
  88.3 1.2 fusion
  89.5 0.7 copy.47
  90.2 0.8 fusion.15
  91.0 2.5 %collective-permute-start = (bf16[256,256]{0,1:T(8,128)(2,1)S(1)}, bf16[256,256]{0,1:T(8,128)(2,1)S(1)}, u32[]{:S(2)}, u32[]{:S(2)}) collective-permute-start(bf16[256,256]{0,1:T(8,128)(2,1)S(1)} %slice_bitcast_fusion), channel_id=1, source_target_pairs={{0,1},{1,2},{2,3},{3,4},{4,5},{5,6},{6,7},{7,8},{8,9},{9,10},{10,1... | collective-permute-start | bytes 393224 | tf_op jit(solution)/shard_map/ppermute | solution.py:14
  93.5 1.7 collective-permute-done
  95.2 0.1 pad_maximum_fusion
  95.3 0.0 copy-start.1
  95.3 0.0 copy-start.2
  95.3 0.0 copy-start.3
  95.3 0.2 multiply_convert_fusion
  95.5 0.9 copy.49
  96.5 0.0 all-gather.2.cloned.1.call-update
  96.5 0.0 copy-done.1
  96.5 0.1 copy.45
  96.6 0.0 copy-done.2
  96.6 0.1 copy.52
  96.7 0.0 copy-done.3
  96.7 0.2 convert_reduce_fusion
  96.9 0.1 select_reduce_fusion
  97.0 0.0 copy-done
  97.0 0.7 gather_fusion
  97.7 0.6 gather_fusion.2
  98.3 0.6 gather_fusion.3
  98.8 0.1 broadcast_select_fusion.1
  98.9 0.2 slice_reduce_fusion.1
  99.1 0.1 copy.54
  99.2 0.1 copy.53
  99.3 0.1 copy.51
  99.4 0.1 copy.50
  99.5 0.1 pad_add_fusion
  99.5 0.1 compare_and_fusion
  99.6 0.1 fusion.66
  99.7 0.1 fusion.59
  99.8 1.0 fusion.37
  100.8 1.0 multiply_convert_fusion.3
  101.8 0.1 broadcast_bitcast_fusion
  101.9 0.1 fusion.57
  102.0 47.4 %all-gather.2.cloned.1.call-done = bf16[48,256,256]{2,1,0:T(8,128)(2,1)} async-done(((bf16[3,256,256]{2,1,0:T(8,128)(2,1)}), bf16[48,256,256]{2,1,0:T(8,128)(2,1)}) %all-gather.2.cloned.1.call-update) | async-done | bytes 6291472 | tf_op jit(solution)/shard_map/all_gather | solution.py:93
  149.4 9.0 %copy.55 = bf16[48,256,256]{2,0,1:T(8,128)(2,1)} copy(bf16[48,256,256]{2,1,0:T(8,128)(2,1)} %all-gather.2.cloned.1.call-done) | data formatting | bytes 12582912 | tf_op jit(solution)/shard_map/all_gather | solution.py:93
  158.4 7.5 %gather_fusion.1 = bf16[24,128,256]{2,0,1:T(8,128)(2,1)S(1)} fusion(bf16[48,256,256]{2,0,1:T(8,128)(2,1)} %copy.55, s32[24]{0:T(128)S(1)} %fusion.66), kind=kCustom, calls=%fused_computation.3 | custom fusion | bytes 3146016 | tf_op jit(solution)/shard_map/vmap()/gather | solution.py:99
  165.8 0.4 copy.56
  166.2 2.4 %fusion.5 = bf16[3072,256]{1,0:T(8,128)(2,1)S(1)} fusion(bf16[24,128,256]{2,1,0:T(8,128)(2,1)S(1)} %copy.56, pred[3072]{0:T(1024)(128)(4,1)S(1)} %broadcast_bitcast_fusion, pred[3072]{0:T(1024)(128)(4,1)S(1)} %fusion.57), kind=kLoop, calls=%fused_computation.14 | loop fusion | flops 1572864 | bytes 3151872 | tf_op jit(solution)/shard_map/jit(_where)/select_n | solution.py:104
  168.6 1.0 convolution_convert_fusion
  169.6 0.8 fusion.10
  170.5 0.8 fusion.12
  171.3 0.8 subtract_bitcast_fusion
  172.1 0.9 add_bitcast_fusion
  173.0 1.2 fusion.21
  174.1 0.8 divide_convert_fusion.1
  175.0 0.6 fusion.50
  175.6 0.6 fusion.52
  176.2 0.6 fusion.17
  176.8 0.6 fusion.16
  177.4 1.5 fusion.18
  (9 shorter events, 0.1 us)
Async XLA Ops:
  6.5 90.5 %copy-start = (s32[64]{0:T(128)S(1)}, s32[64]{0:T(128)}, u32[]{:S(2)}) copy-start(s32[64]{0:T(128)} %param.10) | copy-start | bytes 772
  6.5 81.5 %all-to-all-start = ((bf16[96,32,512]{2,1,0:T(8,128)(2,1)}), bf16[96,32,512]{2,1,0:T(8,128)(2,1)S(1)}, u32[]{:S(2)}, u32[]{:S(2)}) async-start(bf16[96,32,512]{2,1,0:T(8,128)(2,1)} %param.7), calls=%async_computation | async-start | bytes 6291456 | tf_op jit(solution)/shard_map/all_to_all | solution.py:139
  17.0 132.3 %all-gather.2.cloned.1.call-start = ((), (), s32[]{:S(2)}) async-start(), calls=%async_computation.1 | async-start | bytes 6684672 | tf_op jit(solution)/shard_map/all_gather | solution.py:93
  91.0 4.2 %collective-permute-start = (bf16[256,256]{0,1:T(8,128)(2,1)S(1)}, bf16[256,256]{0,1:T(8,128)(2,1)S(1)}, u32[]{:S(2)}, u32[]{:S(2)}) collective-permute-start(bf16[256,256]{0,1:T(8,128)(2,1)S(1)} %slice_bitcast_fusion), channel_id=1, source_target_pairs={{0,1},{1,2},{2,3},{3,4},{4,5},{5,6},{6,7},{7,8},{8,9},{9,10},{10,1... | collective-permute-start | bytes 393224 | tf_op jit(solution)/shard_map/ppermute | solution.py:14
  95.3 1.2 copy-start.1
  95.3 1.3 copy-start.2
  95.3 1.4 copy-start.3
Sparse Core Ops, SparseCore 0:
  96.6 52.7 all-gather.1
where the time goes:
time: 186 us
  waiting for transfers between devices  120 us (65%)
  local copies, waits for them, and re-layouts  21.3 us (11%)
  between operations  13.6 us (7%)
  starting transfers between devices  13 us (7%)
  matrix products  10.2 us (5%)
  other arithmetic  7.53 us (4%)
    all_to_all x1, waiting for transfers between devices, per_device(): lax.all_to_all(raw_planes, 'tile', split_axis=0, concat_axis=1, tiled=True)  70.9 us
    all_gather x1, waiting for transfers between devices, fetch_bands(): shards = lax.all_gather(sections, 'tile', axis=0, tiled=True)  47.4 us
    all_to_all x1, starting transfers between devices, per_device(): lax.all_to_all(raw_planes, 'tile', split_axis=0, concat_axis=1, tiled=True)  10.5 us
    all_gather x1, local copies, waits for them, and re-layouts, fetch_bands(): shards = lax.all_gather(sections, 'tile', axis=0, tiled=True)  9 us
    gather x2, local copies, waits for them, and re-layouts, slice_band(): lax.dynamic_slice(shards, (which, row_start, zero_index), (1, BAND, colum...  7.83 us
  transfers between devices with their start and end apart: 3, of which 3 were waited for; matrix products, arithmetic and copies ran while one was open for 3% of the time, Pallas kernels for 0%

commit v1 on v0

--- a/solution.py
+++ b/solution.py
@@ -90,7 +90,9 @@
     zero_index = jnp.zeros((), jnp.int32)
     blank_bands = jnp.zeros((wanted, BAND, columns), sections.dtype)
     band_index = jnp.arange(BAND, dtype=jnp.int32)
-    shards = lax.all_gather(sections, "tile", axis=0, tiled=True)
+    shards = jnp.concatenate(
+        lax.all_to_all(jnp.stack([sections] * lax.axis_size("tile")), "tile", 0, 0), axis=0
+    )
     held = shards.shape[0]
     inside = (section_ids >= 0) & (section_ids < held)
     clipped = jnp.clip(section_ids, 0, held - 1)

time: 186 us -> 273 us (1.47); the launches traced: 186 us -> 269 us
  waiting for transfers between devices: 120 us -> 206 us
  between operations: 13.6 us -> 0.21 us
  starting transfers between devices: 13 us -> 21.6 us
    all_to_all x0 -> x1, waiting for transfers between devices: none -> 133 us  [fetch_bands(): lax.all_to_all(jnp.stack([sections] * lax.axis_size('tile')), 'tile', 0, 0)]
    all_gather x1 -> x0, waiting for transfers between devices: 47.4 us -> none  [fetch_bands(): shards = lax.all_gather(sections, 'tile', axis=0, tiled=True)]
    reshape x0 -> x1, local copies, waits for them, and re-layouts: none -> 9 us  [fetch_bands(): jnp.concatenate(lax.all_to_all(jnp.stack([sections] * lax.axis_size('tile...]
    all_gather x1 -> x0, local copies, waits for them, and re-layouts: 9 us -> none  [fetch_bands(): shards = lax.all_gather(sections, 'tile', axis=0, tiled=True)]
    all_to_all x0 -> x1, starting transfers between devices: none -> 8.8 us  [fetch_bands(): lax.all_to_all(jnp.stack([sections] * lax.axis_size('tile')), 'tile', 0, 0)]
    another operation x0 -> x1, local copies, waits for them, and re-layouts: none -> 3.4 us  [fetch_bands(): jnp.stack([sections] * lax.axis_size('tile'))]
  transfers between devices with their start and end apart: 3 -> 3, of which waited for: 3 -> 3; matrix products, arithmetic and copies ran while one was open for 3% -> 2% of each run, Pallas kernels for 0% -> 0%
where the time goes in v1:
time: 273 us; the launch traced here: 269 us
  waiting for transfers between devices  206 us (75%)
  local copies, waits for them, and re-layouts  24 us (9%)
  starting transfers between devices  21.6 us (8%)
  matrix products  10.2 us (4%)
  other arithmetic  7.53 us (3%)
    all_to_all x1, waiting for transfers between devices, fetch_bands(): lax.all_to_all(jnp.stack([sections] * lax.axis_size('tile')), 'tile', 0, 0)  133 us
    all_to_all x1, waiting for transfers between devices, per_device(): lax.all_to_all(raw_planes, 'tile', split_axis=0, concat_axis=1, tiled=True)  71 us
    all_to_all x1, starting transfers between devices, per_device(): lax.all_to_all(raw_planes, 'tile', split_axis=0, concat_axis=1, tiled=True)  10.5 us
    reshape x1, local copies, waits for them, and re-layouts, fetch_bands(): jnp.concatenate(lax.all_to_all(jnp.stack([sections] * lax.axis_size('tile...  9 us
    all_to_all x1, starting transfers between devices, fetch_bands(): lax.all_to_all(jnp.stack([sections] * lax.axis_size('tile')), 'tile', 0, 0)  8.8 us
    gather x2, local copies, waits for them, and re-layouts, slice_band(): lax.dynamic_slice(shards, (which, row_start, zero_index), (1, BAND, colum...  7.83 us
  transfers between devices with their start and end apart: 3, of which 3 were waited for; matrix products, arithmetic and copies ran while one was open for 2% of the time, Pallas kernels for 0%

profile of v1, /device:TPU:1, one launch (start us, length us, event | category | flops | bytes accessed | tf_op | source)
XLA Modules:
  0.0 269.4 jit_solution(12854243952144211217)
XLA Ops:
  0.0 0.0 copy-start
  0.0 10.5 %all-to-all-start = ((bf16[96,32,512]{2,1,0:T(8,128)(2,1)}), bf16[96,32,512]{2,1,0:T(8,128)(2,1)S(1)}, u32[]{:S(2)}, u32[]{:S(2)}) async-start(bf16[96,32,512]{2,1,0:T(8,128)(2,1)} %param.7), calls=%async_computation | async-start | bytes 6291456 | tf_op jit(solution)/shard_map/all_to_all | solution.py:141
  10.5 71.0 %all-to-all-done = bf16[96,32,512]{2,1,0:T(8,128)(2,1)S(1)} async-done(((bf16[96,32,512]{2,1,0:T(8,128)(2,1)}), bf16[96,32,512]{2,1,0:T(8,128)(2,1)S(1)}, u32[]{:S(2)}, u32[]{:S(2)}) %all-to-all-start) | async-done | bytes 3145760 | tf_op jit(solution)/shard_map/all_to_all | solution.py:141
  81.5 0.2 copy.48
  81.7 1.2 fusion
  82.9 0.7 copy.49
  83.6 0.8 fusion.15
  84.4 2.3 collective-permute-start
  86.8 1.9 collective-permute-done
  88.7 0.1 pad_maximum_fusion
  88.8 0.2 multiply_convert_fusion
  89.0 0.2 copy.51
  89.1 3.4 %stack.2 = bf16[16,3,256,256]{3,2,1,0:T(8,128)(2,1)} broadcast(bf16[3,256,256]{2,1,0:T(8,128)(2,1)S(1)} %copy.51), dimensions={1,2,3} | broadcast | bytes 6684672 | tf_op jit(solution)/shard_map/stack | solution.py:94
  92.5 0.0 copy-start.1
  92.5 0.0 copy-start.2
  92.5 0.0 copy-start.3
  92.5 8.8 %all-to-all-start.1 = ((bf16[16,3,256,256]{3,2,1,0:T(8,128)(2,1)}), bf16[16,3,256,256]{3,2,1,0:T(8,128)(2,1)}, u32[]{:S(2)}, u32[]{:S(2)}) async-start(bf16[16,3,256,256]{3,2,1,0:T(8,128)(2,1)} %stack.2), calls=%async_computation.1 | async-start | bytes 12582912 | tf_op jit(solution)/shard_map/all_to_all | solution.py:94
  101.3 0.0 copy-done.1
  101.3 0.1 copy.47
  101.4 0.0 copy-done.2
  101.4 0.1 copy.54
  101.5 0.0 copy-done.3
  101.5 0.2 convert_reduce_fusion
  101.7 0.1 select_reduce_fusion
  101.9 0.0 copy-done
  101.9 0.7 gather_fusion
  102.6 0.6 gather_fusion.2
  103.1 0.6 gather_fusion.3
  103.7 0.1 broadcast_select_fusion.1
  103.8 0.2 slice_reduce_fusion.1
  104.0 0.1 copy.56
  104.0 0.1 copy.55
  104.1 0.1 copy.53
  104.2 0.1 copy.52
  104.3 0.1 pad_add_fusion
  104.4 0.1 compare_and_fusion
  104.5 0.1 fusion.66
  104.6 0.1 fusion.59
  104.7 1.0 fusion.37
  105.7 1.0 multiply_convert_fusion.3
  106.7 0.1 broadcast_bitcast_fusion
  106.7 0.1 fusion.57
  106.8 133.0 %all-to-all-done.1 = bf16[16,3,256,256]{3,2,1,0:T(8,128)(2,1)} async-done(((bf16[16,3,256,256]{3,2,1,0:T(8,128)(2,1)}), bf16[16,3,256,256]{3,2,1,0:T(8,128)(2,1)}, u32[]{:S(2)}, u32[]{:S(2)}) %all-to-all-start.1) | async-done | bytes 6291488 | tf_op jit(solution)/shard_map/all_to_all | solution.py:94
  239.8 9.0 %copy.57 = bf16[48,256,256]{2,0,1:T(8,128)(2,1)} copy(bf16[48,256,256]{2,1,0:T(8,128)(2,1)} %bitcast.14) | data formatting | bytes 12582912 | tf_op jit(solution)/shard_map/reshape | solution.py:93
  248.8 7.5 %gather_fusion.1 = bf16[24,128,256]{2,0,1:T(8,128)(2,1)S(1)} fusion(bf16[48,256,256]{2,0,1:T(8,128)(2,1)} %copy.57, s32[24]{0:T(128)S(1)} %fusion.66), kind=kCustom, calls=%fused_computation.3 | custom fusion | bytes 3146016 | tf_op jit(solution)/shard_map/vmap()/gather | solution.py:101
  256.3 0.4 copy.58
  256.6 2.4 fusion.5
  259.1 1.0 convolution_convert_fusion
  260.1 0.8 fusion.10
  260.9 0.8 fusion.12
  261.7 0.8 subtract_bitcast_fusion
  262.6 0.9 add_bitcast_fusion
  263.4 1.2 fusion.21
  264.6 0.8 divide_convert_fusion.1
  265.4 0.6 fusion.50
  266.0 0.6 fusion.52
  266.6 0.6 fusion.17
  267.3 0.6 fusion.16
  267.9 1.5 fusion.18
  (9 shorter events, 0.1 us)
Async XLA Ops:
  0.0 101.9 %copy-start = (s32[64]{0:T(128)S(1)}, s32[64]{0:T(128)}, u32[]{:S(2)}) copy-start(s32[64]{0:T(128)} %param.10) | copy-start | bytes 772
  0.0 81.5 %all-to-all-start = ((bf16[96,32,512]{2,1,0:T(8,128)(2,1)}), bf16[96,32,512]{2,1,0:T(8,128)(2,1)S(1)}, u32[]{:S(2)}, u32[]{:S(2)}) async-start(bf16[96,32,512]{2,1,0:T(8,128)(2,1)} %param.7), calls=%async_computation | async-start | bytes 6291456 | tf_op jit(solution)/shard_map/all_to_all | solution.py:141
  84.4 4.2 %collective-permute-start = (bf16[256,256]{0,1:T(8,128)(2,1)S(1)}, bf16[256,256]{0,1:T(8,128)(2,1)S(1)}, u32[]{:S(2)}, u32[]{:S(2)}) collective-permute-start(bf16[256,256]{0,1:T(8,128)(2,1)S(1)} %slice_bitcast_fusion), channel_id=1, source_target_pairs={{0,1},{1,2},{2,3},{3,4},{4,5},{5,6},{6,7},{7,8},{8,9},{9,10},{10,1... | collective-permute-start | bytes 393224 | tf_op jit(solution)/shard_map/ppermute | solution.py:14
  92.5 8.8 %copy-start.1 = (s32[64,2]{0,1:T(2,128)S(1)}, s32[64,2]{0,1:T(2,128)}, u32[]{:S(2)}) copy-start(s32[64,2]{0,1:T(2,128)} %param.8) | copy-start | bytes 1540
  92.5 8.9 %copy-start.2 = (s32[64,2]{0,1:T(2,128)S(1)}, s32[64,2]{0,1:T(2,128)}, u32[]{:S(2)}) copy-start(s32[64,2]{0,1:T(2,128)} %param.9) | copy-start | bytes 1540
  92.5 9.0 %copy-start.3 = (s32[64,1]{0,1:T(1,128)S(1)}, s32[64,1]{0,1:T(1,128)}, u32[]{:S(2)}) copy-start(s32[64,1]{0,1:T(1,128)} %param.11) | copy-start | bytes 772
  92.5 147.3 %all-to-all-start.1 = ((bf16[16,3,256,256]{3,2,1,0:T(8,128)(2,1)}), bf16[16,3,256,256]{3,2,1,0:T(8,128)(2,1)}, u32[]{:S(2)}, u32[]{:S(2)}) async-start(bf16[16,3,256,256]{3,2,1,0:T(8,128)(2,1)} %stack.2), calls=%async_computation.1 | async-start | bytes 12582912 | tf_op jit(solution)/shard_map/all_to_all | solution.py:94
